TPU v7x, 32 devices: a whole 2x2x4 slice. The times are simulated.
32 devices in a mesh: dp: 2 (over y), ctx: 4 (over z), fsdp: 4 (over x, core).
Axes of the slice: x: 2, y: 2, z: 4, core: 2. Of those that a mesh axis runs over, the one named last changes fastest.
Arguments:
- grad_parts: bfloat16 [2, 2, 512, 16384], P('dp', None, 'fsdp', 'ctx'), may hold values from -6 to 6
- weight: bfloat16 [2, 512, 16384], P('dp', 'fsdp', 'ctx'), may hold values from -0.25 to 0.25
- logit_max: float32 [2, 4, 2, 64], P('dp', 'ctx'), may hold values from 10 to 1000
Outputs:
- update: float32 [2, 512, 16384], P('dp', 'fsdp', 'ctx')
- new_weight: float32 [2, 512, 16384], P('dp', 'fsdp', 'ctx')
All inputs are finite; a program needn't handle non-finite values.
Results may differ from a plain program's by a relative error of at most 0.0003.
Values sent between devices are 32-bit elements; how exact they have to be, the bound alone decides.
A program may use at most 64 MiB of HBM per device.

v0:
```python
import math

import jax
import jax.numpy as jnp
from jax import lax
from jax.sharding import PartitionSpec as P

KV_RANK = 512
HEADS = 64
NOPE = 128
V_DIM = 128
ITERS = 2


ns_a = 3.4445
ns_b = -4.775
ns_c = 2.0315
eps_norm = 1e-07
tau_clip = 100.0
learn_rate = 0.02
decay_rate = 0.1


def matmul(left, right):
    return jnp.dot(left, right, preferred_element_type=jnp.float32, precision=lax.Precision.HIGHEST)


def gram_sum(block):
    local = matmul(block, block.T)
    half = local.shape[0] // 2
    upper, corner = lax.psum((local[:half], local[half:, half:]), ("ctx", "fsdp"))
    lower = jnp.concatenate([upper[:, half:].T, corner], axis=1)
    return jnp.concatenate([upper, lower], axis=0)


def columns_of(head_factor):
    count = head_factor.shape[0]
    keys = jnp.broadcast_to(head_factor[:, None], (count, NOPE))
    values = jnp.ones((count, V_DIM), dtype=head_factor.dtype)
    return jnp.concatenate([keys, values], axis=1).reshape(-1)


def shards(grad_parts, weight, logit_max):
    parts = grad_parts[0].astype(jnp.float32)
    summed = lax.psum_scatter(parts, "dp", scatter_dimension=0, tiled=True)
    owned = lax.all_to_all(summed[0], "fsdp", split_axis=1, concat_axis=0, tiled=True)
    peak = lax.pmax(logit_max, ("dp", "ctx"))
    total_cols = HEADS * (NOPE + V_DIM)
    scale = 0.2 * math.sqrt(max(KV_RANK, total_cols))
    gram_raw = gram_sum(owned)
    norm = jnp.sqrt(jnp.trace(gram_raw))
    denom = norm + eps_norm
    start_x = owned / denom
    gram = gram_raw / (denom * denom)
    iterate = start_x
    for step in range(ITERS):
        if step > 0:
            gram = gram_sum(iterate)
        poly = ns_b * gram + ns_c * matmul(gram, gram)
        iterate = ns_a * iterate + matmul(poly, iterate)
    step_value = scale * iterate
    back = lax.all_to_all(step_value, "fsdp", split_axis=0, concat_axis=1, tiled=True)
    layer_peak = lax.dynamic_index_in_dim(peak[0, 0], lax.axis_index("dp"), 0, keepdims=False)
    heads_here = HEADS // lax.axis_size("ctx")
    local_peak = lax.dynamic_slice_in_dim(
        layer_peak, lax.axis_index("ctx") * heads_here, heads_here, 0
    )
    factor = jnp.sqrt(jnp.minimum(1.0, tau_clip / local_peak))
    column_factor = columns_of(factor)
    fresh = (
        weight[0].astype(jnp.float32) * (1.0 - learn_rate * decay_rate) - learn_rate * back
    ) * column_factor[None, :]
    return (back[None], fresh[None])


def solution(mesh):
    return jax.shard_map(
        shards,
        mesh=mesh,
        in_specs=(P("dp", None, "fsdp", "ctx"), P("dp", "fsdp", "ctx"), P("dp", "ctx", None, None)),
        out_specs=(P("dp", "fsdp", "ctx"), P("dp", "fsdp", "ctx")),
        check_vma=False,
    )
```

profile of v0, /device:TPU:1, one launch (start us, length us, event | category | flops | bytes accessed | tf_op | source)
XLA Modules:
  0.0 358.0 jit_solution(13153257141152846801)
XLA Ops:
  7.2 4.0 %bitcast_convert_fusion = f32[2,128,4096]{2,1,0:T(8,128)} fusion(bf16[1,2,128,4096]{3,2,1,0:T(8,128)(2,1)} %param.3), kind=kLoop, calls=%fused_computation | loop fusion | flops 1048576 | bytes 6291456 | tf_op jit(solution)/shard_map/convert_element_type | solution.py:44
  11.3 56.4 %reduce-scatter.2.cloned.1.call-done = f32[1,128,4096]{2,1,0:T(8,128)} async-done(((f32[2,128,4096]{2,1,0:T(8,128)}), f32[1,128,4096]{2,1,0:T(8,128)}) %reduce-scatter.2.cloned.1.call-update) | async-done | bytes 2097168 | tf_op jit(solution)/shard_map/reduce_scatter | solution.py:45
  67.7 2.7 all_to_all.26
  70.4 1.2 copy.5
  71.6 28.0 %all_to_all.35 = f32[128,4,1024]{2,0,1:T(8,128)S(1)} all-to-all(f32[128,4,1024]{2,0,1:T(8,128)S(1)} %copy.5), channel_id=1, replica_groups=mesh['dp'=2,'ctx'=4,'fsdp'=4] {'fsdp'}, dimensions={1} | all-to-all | bytes 4194304 | tf_op jit(solution)/shard_map/all_to_all | solution.py:46
  99.6 3.5 fusion.8
  104.9 91.4 %all-reduce.8.cloned.1.call-done = (f32[256,256]{1,0:T(8,128)}, f32[256,512]{1,0:T(8,128)}) async-done(((f32[256,256]{1,0:T(8,128)}, f32[256,512]{1,0:T(8,128)}), (f32[256,256]{1,0:T(8,128)}, f32[256,512]{1,0:T(8,128)})) %all-reduce.8.cloned.1.call-update) | async-done | bytes 786448 | tf_op jit(solution)/shard_map/psum | solution.py:31
  196.4 1.0 slice_bitcast_fusion.1
  197.5 1.8 select_reduce_fusion
  200.1 2.0 fusion.2
  202.1 3.6 %multiply_add_fusion = f32[512,1024]{1,0:T(8,128)S(1)} fusion(f32[512,512]{1,0:T(8,128)S(1)} %fusion.2, f32[512,1024]{1,0:T(8,128)S(1)} %bitcast.25, f32[]{:T(128)S(6)} %add.38), kind=kOutput, calls=%fused_computation.3 | convolution fusion | flops 3223322624 | bytes 5242884 | tf_op jit(solution)/shard_map/dot_general | solution.py:25
  205.7 3.5 fusion.9
  210.0 1.0 copy.10
  211.0 92.3 %all-reduce.6.cloned.1.call-done = (f32[256,256]{1,0:T(8,128)}, f32[256,512]{0,1:T(8,128)}) async-done(((f32[256,256]{1,0:T(8,128)}, f32[256,512]{0,1:T(8,128)}), (f32[256,256]{1,0:T(8,128)}, f32[256,512]{0,1:T(8,128)})) %all-reduce.6.cloned.1.call-update) | async-done | bytes 786448 | tf_op jit(solution)/shard_map/psum | solution.py:31
  303.3 1.2 copy.8
  304.5 1.0 slice_bitcast_fusion
  305.5 3.2 fusion.1
  308.7 5.3 %add_multiply_fusion = f32[512,1024]{1,0:T(8,128)} fusion(f32[512,1024]{1,0:T(8,128)S(1)} %copy-done.1, f32[512,512]{1,0:T(8,128)S(1)} %fusion.1), kind=kOutput, calls=%fused_computation.2 | convolution fusion | flops 3222798336 | bytes 5242880 | tf_op jit(solution)/shard_map/dot_general | solution.py:25
  313.9 5.2 %all-to-all-start.1 = ((f32[4,128,1024]{2,1,0:T(8,128)}), f32[4,128,1024]{2,1,0:T(8,128)S(1)}, u32[]{:S(2)}, u32[]{:S(2)}) async-start(f32[4,128,1024]{2,1,0:T(8,128)} %bitcast.27), calls=%async_computation.2 | async-start | bytes 4194304 | tf_op jit(solution)/shard_map/all_to_all | solution.py:62
  319.2 16.6 %pmax.7 = f32[1,1,2,64]{3,2,1,0:T(2,128)S(1)} all-reduce(f32[1,1,2,64]{3,2,1,0:T(2,128)S(1)} %copy-done.6), channel_id=1, replica_groups=mesh['dp'=2,'ctx'=4,'fsdp'=4] {'dp','ctx'}, use_global_device_ids=true, to_apply=%region_6.7 | all-reduce | flops 128 | bytes 1024 | tf_op jit(solution)/shard_map/pmax | solution.py:47
  336.0 7.9 %all-to-all-done.1 = f32[4,128,1024]{2,1,0:T(8,128)S(1)} async-done(((f32[4,128,1024]{2,1,0:T(8,128)}), f32[4,128,1024]{2,1,0:T(8,128)S(1)}, u32[]{:S(2)}, u32[]{:S(2)}) %all-to-all-start.1) | async-done | bytes 2097184 | tf_op jit(solution)/shard_map/all_to_all | solution.py:62
  343.9 2.7 copy.9
  346.6 2.8 broadcast_in_dim.16
  349.4 2.0 subtract_multiply_fusion
  (29 shorter events, 3.0 us)
Async XLA Ops:
  7.2 60.5 %reduce-scatter.2.cloned.1.call-start = ((), (), s32[]{:S(2)}) async-start(), calls=%async_computation.3 | async-start | bytes 6291456 | tf_op jit(solution)/shard_map/reduce_scatter | solution.py:45
  11.3 185.1 %all-reduce.8.cloned.1.call-start = ((), (), s32[]{:S(2)}) async-start(), calls=%async_computation.5 | async-start | bytes 1572864 | tf_op jit(solution)/shard_map/psum | solution.py:31
  104.7 198.5 %all-reduce.6.cloned.1.call-start = ((), (), s32[]{:S(2)}) async-start(), calls=%async_computation.4 | async-start | bytes 1572864 | tf_op jit(solution)/shard_map/psum | solution.py:31
  196.4 3.7 %copy-start.3 = (f32[256,512]{1,0:T(8,128)S(1)}, f32[256,512]{1,0:T(8,128)}, u32[]{:S(2)}) copy-start(f32[256,512]{1,0:T(8,128)} %get-tuple-element.5) | copy-start | bytes 1572868
  196.4 3.7 %copy-start.5 = (f32[256,256]{1,0:T(8,128)S(1)}, f32[256,256]{1,0:T(8,128)}, u32[]{:S(2)}) copy-start(f32[256,256]{1,0:T(8,128)} %get-tuple-element.4) | copy-start | bytes 786436
  205.7 3.6 copy-start
  305.5 3.2 copy-start.1
  313.9 5.2 %copy-start.6 = (f32[1,1,2,64]{3,2,1,0:T(2,128)S(1)}, f32[1,1,2,64]{3,2,1,0:T(2,128)}, u32[]{:S(2)}) copy-start(f32[1,1,2,64]{3,2,1,0:T(2,128)} %param.5) | copy-start | bytes 1540
  313.9 29.9 %all-to-all-start.1 = ((f32[4,128,1024]{2,1,0:T(8,128)}), f32[4,128,1024]{2,1,0:T(8,128)S(1)}, u32[]{:S(2)}, u32[]{:S(2)}) async-start(f32[4,128,1024]{2,1,0:T(8,128)} %bitcast.27), calls=%async_computation.2 | async-start | bytes 4194304 | tf_op jit(solution)/shard_map/all_to_all | solution.py:62
  346.6 2.8 copy-start.4
  349.4 2.1 copy-start.2
Sparse Core Ops, SparseCore 0:
  11.4 56.2 reduce-scatter.1
  104.8 91.4 all-reduce.7
  211.1 92.0 all-reduce.5
where the time goes:
time: 359 us; the launch traced here: 358 us
  waiting for transfers between devices  248 us (69%)
  blocking collectives  44.6 us (12%)
  matrix products  21.1 us (6%)
  local copies, waits for them, and re-layouts  16.1 us (4%)
  between operations  14.6 us (4%)
  other arithmetic  7.95 us (2%)
  starting transfers between devices  5.54 us (2%)
    psum x2, waiting for transfers between devices, gram_sum(): lax.psum((local[:half], local[half:, half:]), ('ctx', 'fsdp'))  184 us
    reduce_scatter x1, waiting for transfers between devices, shards(): summed = lax.psum_scatter(parts, 'dp', scatter_dimension=0, tiled=True)  56.4 us
    all_to_all x1, blocking collectives, shards(): lax.all_to_all(summed[0], 'fsdp', split_axis=1, concat_axis=0, tiled=True)  28 us
    dot_general x6, matrix products, matmul(): jnp.dot(left, right, preferred_element_type=jnp.float32, precision=lax.Pr...  21.1 us
    pmax x1, blocking collectives, shards(): peak = lax.pmax(logit_max, ('dp', 'ctx'))  16.6 us
    all_to_all x1, waiting for transfers between devices, shards(): lax.all_to_all(step_value, 'fsdp', split_axis=0, concat_axis=1, tiled=True)  7.87 us
  transfers between devices with their start and end apart: 4, of which 4 were waited for; matrix products, arithmetic and copies ran while one was open for 0% of the time, Pallas kernels for 0%

commit v1 on v0

--- a/solution.py
+++ b/solution.py
@@ -1,8 +1,11 @@
+import functools
 import math
 
 import jax
 import jax.numpy as jnp
 from jax import lax
+from jax.experimental import pallas as pl
+from jax.experimental.pallas import tpu as pltpu
 from jax.sharding import PartitionSpec as P
 
 KV_RANK = 512
@@ -20,6 +23,12 @@
 learn_rate = 0.02
 decay_rate = 0.1
 
+HEAD_COLS = NOPE + V_DIM
+BLOCK = 128
+SIDE = KV_RANK // BLOCK
+PAIRS = [(i, j) for i in range(SIDE) for j in range(i, SIDE)]
+UPDATE_SCALE = 0.2 * math.sqrt(max(KV_RANK, HEADS * HEAD_COLS))
+
 
 def matmul(left, right):
     return jnp.dot(left, right, preferred_element_type=jnp.float32, precision=lax.Precision.HIGHEST)
@@ -45,20 +54,16 @@
     summed = lax.psum_scatter(parts, "dp", scatter_dimension=0, tiled=True)
     owned = lax.all_to_all(summed[0], "fsdp", split_axis=1, concat_axis=0, tiled=True)
     peak = lax.pmax(logit_max, ("dp", "ctx"))
-    total_cols = HEADS * (NOPE + V_DIM)
-    scale = 0.2 * math.sqrt(max(KV_RANK, total_cols))
     gram_raw = gram_sum(owned)
-    norm = jnp.sqrt(jnp.trace(gram_raw))
-    denom = norm + eps_norm
-    start_x = owned / denom
+    denom = jnp.sqrt(jnp.trace(gram_raw)) + eps_norm
+    iterate = owned / denom
     gram = gram_raw / (denom * denom)
-    iterate = start_x
     for step in range(ITERS):
         if step > 0:
             gram = gram_sum(iterate)
         poly = ns_b * gram + ns_c * matmul(gram, gram)
         iterate = ns_a * iterate + matmul(poly, iterate)
-    step_value = scale * iterate
+    step_value = UPDATE_SCALE * iterate
     back = lax.all_to_all(step_value, "fsdp", split_axis=0, concat_axis=1, tiled=True)
     layer_peak = lax.dynamic_index_in_dim(peak[0, 0], lax.axis_index("dp"), 0, keepdims=False)
     heads_here = HEADS // lax.axis_size("ctx")
@@ -73,9 +78,366 @@
     return (back[None], fresh[None])
 
 
+def split(value):
+    high = value.astype(jnp.bfloat16)
+    low = (value - high.astype(jnp.float32)).astype(jnp.bfloat16)
+    return high, low
+
+
+def dot(left, right):
+    return jnp.dot(left, right, preferred_element_type=jnp.float32)
+
+
+def dot_nt(left, right):
+    return lax.dot_general(
+        left, right, (((1,), (1,)), ((), ())), preferred_element_type=jnp.float32
+    )
+
+
+def product(left, right):
+    (lh, ll), (rh, rl) = left, right
+    return dot(lh, rh) + (dot(lh, rl) + dot(ll, rh))
+
+
+def gather_kernel(
+    n_ctx, chunks,
+    grad, logit, x_high, x_low, t_high, t_low, factor,
+    outgoing, arriving, x_all, high_all, low_all, main, cross,
+    packed, partial, total, gram, own_peak, peaks,
+    y_send, y_recv, x_send, x_recv, c_send, c_recv, r_send, r_recv, out_sem,
+    rs_send, rs_recv, ag_send, ag_recv, gx_send, gx_recv, gc_send, gc_recv, gr_send, gr_recv,
+    pk_send, pk_recv,
+):
+    dp = lax.axis_index("dp")
+    ctx = lax.axis_index("ctx")
+    row = lax.axis_index("fsdp")
+    other_dp = 1 - dp
+    across = lax.rem(row + 2, 4)
+    beside = row + 1 - 2 * lax.rem(row, 2)
+    diagonal = lax.rem(beside + 2, 4)
+    rows = grad.shape[1]
+
+    def device(d, c, f):
+        return {"dp": d, "ctx": c, "fsdp": f}
+
+    def send(src, dst, send_sem, recv_sem, where):
+        return pltpu.make_async_remote_copy(
+            src_ref=src, dst_ref=dst, send_sem=send_sem, recv_sem=recv_sem,
+            device_id=where, device_id_type=pl.DeviceIdType.MESH,
+        )
+
+    same = [
+        (e, d) for e in range(2) for d in range(n_ctx) if (e, d) != (0, 0)
+    ]
+
+    def shifted(e, d):
+        return device(lax.rem(dp + e, 2), lax.rem(ctx + d, n_ctx), row)
+
+    barrier = pltpu.get_barrier_semaphore()
+    for e, d in same:
+        pl.semaphore_signal(barrier, 1, device_id=shifted(e, d), device_id_type=pl.DeviceIdType.MESH)
+    for f in (across, beside):
+        pl.semaphore_signal(barrier, 1, device_id=device(dp, ctx, f), device_id_type=pl.DeviceIdType.MESH)
+    own_peak[...] = jnp.full(own_peak.shape, 10.0, jnp.float32)
+    own_peak[0 : logit.shape[0], 0 : logit.shape[1]] = logit[...]
+    pl.semaphore_wait(barrier, len(same) + 2)
+
+    def block_of(f):
+        return pl.ds(pl.multiple_of(f * rows, rows), rows)
+
+    def y_copy(k):
+        return send(
+            outgoing.at[k], arriving.at[k], y_send.at[k], y_recv.at[k], device(other_dp, ctx, row)
+        )
+
+    def x_copy(k, f):
+        part = x_all.at[k, block_of(f)]
+        return send(part, part, x_send.at[k], x_recv.at[k], device(dp, ctx, across))
+
+    def c_copy(k, f):
+        part = x_all.at[k, block_of(f)]
+        return send(part, part, c_send.at[k], c_recv.at[k], device(dp, ctx, beside))
+
+    def r_copy(k, f):
+        part = x_all.at[k, block_of(f)]
+        return send(part, part, r_send.at[k], r_recv.at[k], device(dp, ctx, beside))
+
+    def columns(k):
+        return pl.ds(pl.multiple_of(k * HEAD_COLS, HEAD_COLS), HEAD_COLS)
+
+    def out_copies(k):
+        return (
+            pltpu.make_async_copy(high_all.at[k], x_high.at[k], out_sem.at[0, k]),
+            pltpu.make_async_copy(low_all.at[k], x_low.at[k], out_sem.at[1, k]),
+        )
+
+    def first(k, carry):
+        @pl.when(k < chunks)
+        def _():
+            outgoing[k] = grad[other_dp, :, columns(k)].astype(jnp.float32)
+
+        @pl.when(k >= 1)
+        def _():
+            y_copy(k - 1).start()
+
+        return carry
+
+    lax.fori_loop(0, chunks + 1, first, 0)
+
+    def peak_copy(slot, e, d):
+        return send(own_peak, peaks.at[slot], pk_send.at[slot], pk_recv.at[slot], shifted(e, d))
+
+    for slot, (e, d) in enumerate(same):
+        peak_copy(slot, e, d).start()
+
+    main[...] = jnp.zeros_like(main)
+    cross[...] = jnp.zeros_like(cross)
+
+    def step(s, carry):
+        @pl.when(s < chunks)
+        def _():
+            y_copy(s).wait_recv()
+            x_all[s, block_of(row)] = (
+                grad[dp, :, columns(s)].astype(jnp.float32) + arriving[s]
+            )
+            x_copy(s, row).start()
+            c_copy(s, row).start()
+
+        @pl.when((s >= 2) & (s < chunks + 2))
+        def _():
+            k = s - 2
+            x_copy(k, across).wait_recv()
+            r_copy(k, across).start()
+
+        @pl.when(s >= 3)
+        def _():
+            k = s - 3
+            c_copy(k, beside).wait_recv()
+            r_copy(k, diagonal).wait_recv()
+            high, low = split(x_all[k])
+            high_all[k] = high
+            low_all[k] = low
+            main[...] += dot_nt(high, high)
+            cross[...] += dot_nt(high, low)
+            for copy in out_copies(k):
+                copy.start()
+
+        return carry
+
+    lax.fori_loop(0, chunks + 3, step, 0)
+
+    def tile(ref, i, j):
+        return ref[i * BLOCK : (i + 1) * BLOCK, j * BLOCK : (j + 1) * BLOCK]
+
+    for b, (i, j) in enumerate(PAIRS):
+        packed[b * BLOCK : (b + 1) * BLOCK] = (
+            tile(main, i, j) + tile(cross, i, j) + tile(cross, j, i).T
+        )
+
+    piece = len(PAIRS) * BLOCK // (4 * n_ctx)
+
+    def piece_of(f, c):
+        return pl.ds(pl.multiple_of((f * n_ctx + c) * piece, 8), piece)
+
+    def ahead(d):
+        return lax.rem(ctx + d, n_ctx)
+
+    def behind(d):
+        return lax.rem(ctx + n_ctx - d, n_ctx)
+
+    def rs_copy(d):
+        return send(
+            packed.at[piece_of(row, ahead(d))], partial.at[d],
+            rs_send.at[d], rs_recv.at[d], device(dp, ahead(d), row),
+        )
+
+    for d in range(1, n_ctx):
+        rs_copy(d).start()
+    mine = packed[piece_of(row, ctx)]
+    for d in range(1, n_ctx):
+        rs_copy(d).wait_recv()
+        mine = mine + partial[d]
+    total[piece_of(row, ctx)] = mine
+
+    def ag_copy(d, c):
+        part = total.at[piece_of(row, c)]
+        return send(part, part, ag_send.at[d], ag_recv.at[d], device(dp, ahead(d), row))
+
+    def gx_copy(d, f):
+        part = total.at[piece_of(f, behind(d))]
+        return send(part, part, gx_send.at[d], gx_recv.at[d], device(dp, ctx, across))
+
+    def gc_copy(d, f):
+        part = total.at[piece_of(f, behind(d))]
+        return send(part, part, gc_send.at[d], gc_recv.at[d], device(dp, ctx, beside))
+
+    def gr_copy(d, f):
+        part = total.at[piece_of(f, behind(d))]
+        return send(part, part, gr_send.at[d], gr_recv.at[d], device(dp, ctx, beside))
+
+    for d in range(1, n_ctx):
+        ag_copy(d, ctx).start()
+    for d in range(n_ctx):
+        if d > 0:
+            ag_copy(d, behind(d)).wait_recv()
+        gx_copy(d, row).start()
+        gc_copy(d, row).start()
+    for d in range(n_ctx):
+        gx_copy(d, across).wait_recv()
+        gr_copy(d, across).start()
+
+    top = own_peak[...]
+    for slot, (e, d) in enumerate(same):
+        peak_copy(slot, e, d).wait_recv()
+        top = jnp.maximum(top, peaks[slot])
+    factor[...] = jnp.sqrt(jnp.minimum(1.0, tau_clip / top))
+
+    for d in range(n_ctx):
+        gc_copy(d, beside).wait_recv()
+        gr_copy(d, diagonal).wait_recv()
+
+    near = lax.broadcasted_iota(jnp.int32, (BLOCK, BLOCK), 0) == lax.broadcasted_iota(
+        jnp.int32, (BLOCK, BLOCK), 1
+    )
+    diag = jnp.zeros((BLOCK, BLOCK), jnp.float32)
+    for b, (i, j) in enumerate(PAIRS):
+        if i == j:
+            diag = diag + jnp.where(near, total[b * BLOCK : (b + 1) * BLOCK], 0.0)
+    trace = jnp.sum(jnp.sum(diag, axis=0, keepdims=True), axis=1, keepdims=True)
+    denom = jnp.sqrt(trace) + eps_norm
+    squared = denom * denom
+    for b, (i, j) in enumerate(PAIRS):
+        value = total[b * BLOCK : (b + 1) * BLOCK] / squared
+        gram[i * BLOCK : (i + 1) * BLOCK, j * BLOCK : (j + 1) * BLOCK] = value
+        if i != j:
+            gram[j * BLOCK : (j + 1) * BLOCK, i * BLOCK : (i + 1) * BLOCK] = value.T
+
+    eye = lax.broadcasted_iota(jnp.int32, gram.shape, 0) == lax.broadcasted_iota(
+        jnp.int32, gram.shape, 1
+    )
+    g = gram[...]
+    g_parts = split(g)
+    poly = ns_b * g + ns_c * product(g_parts, g_parts)
+    q0_parts = split(poly + jnp.where(eye, ns_a, 0.0))
+    later = product(split(product(g_parts, q0_parts)), q0_parts)
+    gram[...] = later
+    some = gram[block_of(row)]
+    spot = lax.broadcasted_iota(jnp.int32, some.shape, 0) + row * rows == lax.broadcasted_iota(
+        jnp.int32, some.shape, 1
+    )
+    poly = ns_b * some + ns_c * product(split(some), split(later))
+    q1 = poly + jnp.where(spot, ns_a, 0.0)
+    t = product(split(q1), q0_parts) * (UPDATE_SCALE / denom)
+    high, low = split(t)
+    t_high[...] = high
+    t_low[...] = low
+
+    def last(k, carry):
+        y_copy(k).wait_send()
+        x_copy(k, row).wait_send()
+        c_copy(k, row).wait_send()
+        r_copy(k, across).wait_send()
+        for copy in out_copies(k):
+            copy.wait()
+        return carry
+
+    lax.fori_loop(0, chunks, last, 0)
+    for slot, (e, d) in enumerate(same):
+        peak_copy(slot, e, d).wait_send()
+    for d in range(n_ctx):
+        if d > 0:
+            rs_copy(d).wait_send()
+            ag_copy(d, ctx).wait_send()
+        gx_copy(d, row).wait_send()
+        gc_copy(d, row).wait_send()
+        gr_copy(d, across).wait_send()
+
+
+def gather(grad, logit, n_ctx):
+    _, rows, cols = grad.shape
+    chunks = cols // HEAD_COLS
+    f32, bf16 = jnp.float32, jnp.bfloat16
+    sem = pltpu.SemaphoreType.DMA
+    packed_rows = len(PAIRS) * BLOCK
+    vmem = pl.BlockSpec(memory_space=pltpu.VMEM)
+    anywhere = pl.BlockSpec(memory_space=pl.ANY)
+    wide = (chunks, KV_RANK, HEAD_COLS)
+    return pl.pallas_call(
+        functools.partial(gather_kernel, n_ctx, chunks),
+        out_shape=(
+            jax.ShapeDtypeStruct(wide, bf16),
+            jax.ShapeDtypeStruct(wide, bf16),
+            jax.ShapeDtypeStruct((rows, KV_RANK), bf16),
+            jax.ShapeDtypeStruct((rows, KV_RANK), bf16),
+            jax.ShapeDtypeStruct((8, 128), f32),
+        ),
+        in_specs=[vmem, vmem],
+        out_specs=(anywhere, anywhere, vmem, vmem, vmem),
+        scratch_shapes=[
+            pltpu.VMEM((chunks, rows, HEAD_COLS), f32),
+            pltpu.VMEM((chunks, rows, HEAD_COLS), f32),
+            pltpu.VMEM(wide, f32),
+            pltpu.VMEM(wide, bf16),
+            pltpu.VMEM(wide, bf16),
+            pltpu.VMEM((KV_RANK, KV_RANK), f32),
+            pltpu.VMEM((KV_RANK, KV_RANK), f32),
+            pltpu.VMEM((packed_rows, BLOCK), f32),
+            pltpu.VMEM((n_ctx, packed_rows // (4 * n_ctx), BLOCK), f32),
+            pltpu.VMEM((packed_rows, BLOCK), f32),
+            pltpu.VMEM((KV_RANK, KV_RANK), f32),
+            pltpu.VMEM((8, 128), f32),
+            pltpu.VMEM((2 * n_ctx - 1, 8, 128), f32),
+        ]
+        + [sem((chunks,))] * 8
+        + [sem((2, chunks))]
+        + [sem((n_ctx,))] * 10
+        + [sem((2 * n_ctx - 1,))] * 2,
+        compiler_params=pltpu.CompilerParams(
+            collective_id=0, has_side_effects=True, vmem_limit_bytes=56 * 1024 * 1024
+        ),
+    )(grad, logit)
+
+
+def apply_kernel(heads, factor, t_high, t_low, x_high, x_low, weight, update, fresh):
+    layer = lax.axis_index("dp")
+    base = lax.axis_index("ctx") * (heads * pl.num_programs(0)) + pl.program_id(0) * heads
+    keep = 1.0 - learn_rate * decay_rate
+    for h in range(heads):
+        value = product((t_high[...], t_low[...]), (x_high[h], x_low[h]))
+        start = h * HEAD_COLS
+        update[0, :, start : start + HEAD_COLS] = value
+        old = weight[0, :, start : start + HEAD_COLS].astype(jnp.float32)
+        moved = old * keep - learn_rate * value
+        fresh[0, :, start : start + NOPE] = moved[:, :NOPE] * factor[layer, base + h]
+        fresh[0, :, start + NOPE : start + HEAD_COLS] = moved[:, NOPE:]
+
+
+def apply(factor, t_high, t_low, x_high, x_low, weight, heads):
+    chunks = x_high.shape[0]
+    rows = weight.shape[1]
+    shape = jax.ShapeDtypeStruct(weight.shape, jnp.float32)
+    whole = pl.BlockSpec((rows, KV_RANK), lambda i: (0, 0))
+    stream = pl.BlockSpec((heads, KV_RANK, HEAD_COLS), lambda i: (i, 0, 0))
+    flat = pl.BlockSpec((1, rows, heads * HEAD_COLS), lambda i: (0, 0, i))
+    return pl.pallas_call(
+        functools.partial(apply_kernel, heads),
+        grid=(chunks // heads,),
+        out_shape=(shape, shape),
+        in_specs=[pl.BlockSpec(memory_space=pltpu.SMEM), whole, whole, stream, stream, flat],
+        out_specs=(flat, flat),
+    )(factor, t_high, t_low, x_high, x_low, weight)
+
+
+def kernel_shards(n_ctx, grad_parts, weight, logit_max):
+    x_high, x_low, t_high, t_low, factor = gather(grad_parts[0], logit_max[0, 0], n_ctx)
+    return apply(factor, t_high, t_low, x_high, x_low, weight, 2)
+
+
 def solution(mesh):
+    fits = mesh.shape["dp"] == 2 and mesh.shape["fsdp"] == 4 and mesh.shape["ctx"] <= 8
+    body = functools.partial(kernel_shards, mesh.shape["ctx"]) if fits else shards
     return jax.shard_map(
-        shards,
+        body,
         mesh=mesh,
         in_specs=(P("dp", None, "fsdp", "ctx"), P("dp", "fsdp", "ctx"), P("dp", "ctx", None, None)),
         out_specs=(P("dp", "fsdp", "ctx"), P("dp", "fsdp", "ctx")),

time: 359 us -> 91.7 us (0.26)
  waiting for transfers between devices: 248 us -> 0 us
  Pallas kernels: 0 us -> 90.7 us
  blocking collectives: 44.6 us -> 0 us
  matrix products: 21.1 us -> 0 us
  local copies, waits for them, and re-layouts: 16.1 us -> 0 us
  between operations: 14.6 us -> 0.64 us
  other arithmetic: 7.95 us -> 0 us
  starting transfers between devices: 5.54 us -> 0 us
    psum x2 -> x0, waiting for transfers between devices: 184 us -> none  [gram_sum(): lax.psum((local[:half], local[half:, half:]), ('ctx', 'fsdp'))]
    pallas_call x0 -> x2, Pallas kernels: none -> 90.7 us  [the longest x1 81.6 us: gather(): pl.pallas_call(functools.partial(gather_kernel, n_ctx, chunks), out_shape...]
    reduce_scatter x1 -> x0, waiting for transfers between devices: 56.4 us -> none  [shards(): summed = lax.psum_scatter(parts, 'dp', scatter_dimension=0, tiled=True)]
    all_to_all x1 -> x0, blocking collectives: 28 us -> none  [shards(): lax.all_to_all(summed[0], 'fsdp', split_axis=1, concat_axis=0, tiled=True)]
    dot_general x6 -> x0, matrix products: 21.1 us -> none  [matmul(): jnp.dot(left, right, preferred_element_type=jnp.float32, precision=lax.Pr...]
    pmax x1 -> x0, blocking collectives: 16.6 us -> none  [shards(): peak = lax.pmax(logit_max, ('dp', 'ctx'))]
    all_to_all x1 -> x0, waiting for transfers between devices: 7.87 us -> none  [shards(): lax.all_to_all(step_value, 'fsdp', split_axis=0, concat_axis=1, tiled=True)]
    all_to_all x3 -> x0, local copies, waits for them, and re-layouts: 6.56 us -> none  [the longest x2 3.89 us: shards(): lax.all_to_all(summed[0], 'fsdp', split_axis=1, concat_axis=0, tiled=True)]
  transfers between devices with their start and end apart: 4 -> 0, of which waited for: 4 -> 0; matrix products, arithmetic and copies ran while one was open for 0% -> 0% of each run, Pallas kernels for 0% -> 0%
where the time goes in v1:
time: 91.7 us; the launch traced here: 91.4 us
  Pallas kernels  90.7 us (99%)
    pallas_call x1, Pallas kernels, gather(): pl.pallas_call(functools.partial(gather_kernel, n_ctx, chunks), out_shape...  81.6 us
    pallas_call x1, Pallas kernels, apply(): pl.pallas_call(functools.partial(apply_kernel, heads), grid=(chunks // he...  9.17 us

profile of v1, /device:TPU:1, one launch (start us, length us, event | category | flops | bytes accessed | tf_op | source)
XLA Modules:
  0.0 91.4 jit_solution(17107045454770947180)
XLA Ops:
  0.6 81.6 %shard_map.50 = (bf16[16,512,256]{2,1,0:T(8,128)(2,1)}, bf16[16,512,256]{2,1,0:T(8,128)(2,1)}, bf16[128,512]{1,0:T(8,128)(2,1)}, bf16[128,512]{1,0:T(8,128)(2,1)}, f32[8,128]{1,0:T(8,128)}) custom-call(bf16[2,128,4096]{2,1,0:T(8,128)(2,1)} %bitcast.2, f32[2,64]{1,0:T(2,128)} %bitcast.3), custom_call_target="tpu_custom_call" | custom-call | tf_op jit(solution)/shard_map/pallas_call | solution.py:365
  82.2 9.2 %shard_map.51 = (f32[1,128,4096]{2,1,0:T(8,128)}, f32[1,128,4096]{2,1,0:T(8,128)}) custom-call(f32[8,128]{1,0:T(8,128)} %get-tuple-element.7.factor, bf16[128,512]{1,0:T(8,128)(2,1)} %get-tuple-element.8.t_high, bf16[128,512]{1,0:T(8,128)(2,1)} %get-tuple-element.9.t_low, bf16[16,512,256]{2,1,0:T(8,128)(2,1)} %get-tuple-element.10.x_high, ...), custom_call_target="tpu_custom_call" | custom-call | tf_op jit(solution)/shard_map/pallas_call | solution.py:422

commit v2 on v1

--- a/solution.py
+++ b/solution.py
@@ -25,6 +25,9 @@
 
 HEAD_COLS = NOPE + V_DIM
 BLOCK = 128
+CHUNK = 128
+CUTS = 2
+JOIN = HEAD_COLS // CHUNK
 SIDE = KV_RANK // BLOCK
 PAIRS = [(i, j) for i in range(SIDE) for j in range(i, SIDE)]
 UPDATE_SCALE = 0.2 * math.sqrt(max(KV_RANK, HEADS * HEAD_COLS))
@@ -100,13 +103,13 @@
 
 
 def gather_kernel(
-    n_ctx, chunks,
+    n_ctx, chunks, cuts,
     grad, logit, x_high, x_low, t_high, t_low, factor,
-    outgoing, arriving, x_all, high_all, low_all, main, cross,
+    grads, outgoing, arriving, x_all, high_all, low_all, main, cross,
     packed, partial, total, gram, own_peak, peaks,
     y_send, y_recv, x_send, x_recv, c_send, c_recv, r_send, r_recv, out_sem,
     rs_send, rs_recv, ag_send, ag_recv, gx_send, gx_recv, gc_send, gc_recv, gr_send, gr_recv,
-    pk_send, pk_recv,
+    pk_send, pk_recv, in_sem,
 ):
     dp = lax.axis_index("dp")
     ctx = lax.axis_index("ctx")
@@ -116,6 +119,12 @@
     beside = row + 1 - 2 * lax.rem(row, 2)
     diagonal = lax.rem(beside + 2, 4)
     rows = grad.shape[1]
+    loads = [
+        pltpu.make_async_copy(grad.at[layer], grads.at[layer], in_sem.at[i])
+        for i, layer in enumerate((other_dp, dp))
+    ]
+    for load in loads:
+        load.start()
 
     def device(d, c, f):
         return {"dp": d, "ctx": c, "fsdp": f}
@@ -163,7 +172,7 @@
         return send(part, part, r_send.at[k], r_recv.at[k], device(dp, ctx, beside))
 
     def columns(k):
-        return pl.ds(pl.multiple_of(k * HEAD_COLS, HEAD_COLS), HEAD_COLS)
+        return pl.ds(pl.multiple_of(k * CHUNK, CHUNK), CHUNK)
 
     def out_copies(k):
         return (
@@ -174,7 +183,7 @@
     def first(k, carry):
         @pl.when(k < chunks)
         def _():
-            outgoing[k] = grad[other_dp, :, columns(k)].astype(jnp.float32)
+            outgoing[k] = grads[other_dp, :, columns(k)].astype(jnp.float32)
 
         @pl.when(k >= 1)
         def _():
@@ -182,6 +191,7 @@
 
         return carry
 
+    loads[0].wait()
     lax.fori_loop(0, chunks + 1, first, 0)
 
     def peak_copy(slot, e, d):
@@ -192,13 +202,15 @@
 
     main[...] = jnp.zeros_like(main)
     cross[...] = jnp.zeros_like(cross)
+
+    loads[1].wait()
 
     def step(s, carry):
         @pl.when(s < chunks)
         def _():
             y_copy(s).wait_recv()
             x_all[s, block_of(row)] = (
-                grad[dp, :, columns(s)].astype(jnp.float32) + arriving[s]
+                grads[dp, :, columns(s)].astype(jnp.float32) + arriving[s]
             )
             x_copy(s, row).start()
             c_copy(s, row).start()
@@ -214,13 +226,20 @@
             k = s - 3
             c_copy(k, beside).wait_recv()
             r_copy(k, diagonal).wait_recv()
-            high, low = split(x_all[k])
-            high_all[k] = high
-            low_all[k] = low
-            main[...] += dot_nt(high, high)
-            cross[...] += dot_nt(high, low)
-            for copy in out_copies(k):
-                copy.start()
+
+            @pl.when(lax.rem(k, JOIN) == JOIN - 1)
+            def _():
+                head = lax.div(k, JOIN)
+                value = jnp.concatenate(
+                    [x_all[head * JOIN + i] for i in range(JOIN)], axis=1
+                )
+                high, low = split(value)
+                high_all[head] = high
+                low_all[head] = low
+                main[...] += dot_nt(high, high)
+                cross[...] += dot_nt(high, low)
+                for copy in out_copies(head):
+                    copy.start()
 
         return carry
 
@@ -229,15 +248,23 @@
     def tile(ref, i, j):
         return ref[i * BLOCK : (i + 1) * BLOCK, j * BLOCK : (j + 1) * BLOCK]
 
-    for b, (i, j) in enumerate(PAIRS):
-        packed[b * BLOCK : (b + 1) * BLOCK] = (
-            tile(main, i, j) + tile(cross, i, j) + tile(cross, j, i).T
-        )
-
-    piece = len(PAIRS) * BLOCK // (4 * n_ctx)
-
-    def piece_of(f, c):
-        return pl.ds(pl.multiple_of((f * n_ctx + c) * piece, 8), piece)
+    quarter = len(PAIRS) * BLOCK // 4
+    for f in range(4):
+
+        @pl.when(row == f)
+        def _(f=f):
+            for b, (i, j) in enumerate(PAIRS):
+                if b * BLOCK < (f + 1) * quarter and (b + 1) * BLOCK > f * quarter:
+                    packed[b * BLOCK : (b + 1) * BLOCK] = (
+                        tile(main, i, j) + tile(cross, i, j) + tile(cross, j, i).T
+                    )
+
+    piece = quarter // n_ctx
+    part_rows = piece // cuts
+
+    def piece_of(f, c, h):
+        start = (f * n_ctx + c) * piece + h * part_rows
+        return pl.ds(pl.multiple_of(start, 8), part_rows)
 
     def ahead(d):
         return lax.rem(ctx + d, n_ctx)
@@ -245,46 +272,55 @@
     def behind(d):
         return lax.rem(ctx + n_ctx - d, n_ctx)
 
-    def rs_copy(d):
+    def rs_copy(h, d):
+        n = h * n_ctx + d
         return send(
-            packed.at[piece_of(row, ahead(d))], partial.at[d],
-            rs_send.at[d], rs_recv.at[d], device(dp, ahead(d), row),
+            packed.at[piece_of(row, ahead(d), h)], partial.at[n],
+            rs_send.at[n], rs_recv.at[n], device(dp, ahead(d), row),
         )
 
-    for d in range(1, n_ctx):
-        rs_copy(d).start()
-    mine = packed[piece_of(row, ctx)]
-    for d in range(1, n_ctx):
-        rs_copy(d).wait_recv()
-        mine = mine + partial[d]
-    total[piece_of(row, ctx)] = mine
-
-    def ag_copy(d, c):
-        part = total.at[piece_of(row, c)]
-        return send(part, part, ag_send.at[d], ag_recv.at[d], device(dp, ahead(d), row))
-
-    def gx_copy(d, f):
-        part = total.at[piece_of(f, behind(d))]
-        return send(part, part, gx_send.at[d], gx_recv.at[d], device(dp, ctx, across))
-
-    def gc_copy(d, f):
-        part = total.at[piece_of(f, behind(d))]
-        return send(part, part, gc_send.at[d], gc_recv.at[d], device(dp, ctx, beside))
-
-    def gr_copy(d, f):
-        part = total.at[piece_of(f, behind(d))]
-        return send(part, part, gr_send.at[d], gr_recv.at[d], device(dp, ctx, beside))
-
-    for d in range(1, n_ctx):
-        ag_copy(d, ctx).start()
-    for d in range(n_ctx):
-        if d > 0:
-            ag_copy(d, behind(d)).wait_recv()
-        gx_copy(d, row).start()
-        gc_copy(d, row).start()
-    for d in range(n_ctx):
-        gx_copy(d, across).wait_recv()
-        gr_copy(d, across).start()
+    def ag_copy(h, d, c):
+        n = h * n_ctx + d
+        part = total.at[piece_of(row, c, h)]
+        return send(part, part, ag_send.at[n], ag_recv.at[n], device(dp, ahead(d), row))
+
+    def gx_copy(h, d, f):
+        n = h * n_ctx + d
+        part = total.at[piece_of(f, behind(d), h)]
+        return send(part, part, gx_send.at[n], gx_recv.at[n], device(dp, ctx, across))
+
+    def gc_copy(h, d, f):
+        n = h * n_ctx + d
+        part = total.at[piece_of(f, behind(d), h)]
+        return send(part, part, gc_send.at[n], gc_recv.at[n], device(dp, ctx, beside))
+
+    def gr_copy(h, d, f):
+        n = h * n_ctx + d
+        part = total.at[piece_of(f, behind(d), h)]
+        return send(part, part, gr_send.at[n], gr_recv.at[n], device(dp, ctx, beside))
+
+    for h in range(cuts):
+        for d in range(1, n_ctx):
+            rs_copy(h, d).start()
+    for h in range(cuts):
+        mine = packed[piece_of(row, ctx, h)]
+        for d in range(1, n_ctx):
+            rs_copy(h, d).wait_recv()
+            mine = mine + partial[h * n_ctx + d]
+        total[piece_of(row, ctx, h)] = mine
+        for d in range(1, n_ctx):
+            ag_copy(h, d, ctx).start()
+        gx_copy(h, 0, row).start()
+        gc_copy(h, 0, row).start()
+    for h in range(cuts):
+        for d in range(1, n_ctx):
+            ag_copy(h, d, behind(d)).wait_recv()
+            gx_copy(h, d, row).start()
+            gc_copy(h, d, row).start()
+    for h in range(cuts):
+        for d in range(n_ctx):
+            gx_copy(h, d, across).wait_recv()
+            gr_copy(h, d, across).start()
 
     top = own_peak[...]
     for slot, (e, d) in enumerate(same):
@@ -292,9 +328,10 @@
         top = jnp.maximum(top, peaks[slot])
     factor[...] = jnp.sqrt(jnp.minimum(1.0, tau_clip / top))
 
-    for d in range(n_ctx):
-        gc_copy(d, beside).wait_recv()
-        gr_copy(d, diagonal).wait_recv()
+    for h in range(cuts):
+        for d in range(n_ctx):
+            gc_copy(h, d, beside).wait_recv()
+            gr_copy(h, d, diagonal).wait_recv()
 
     near = lax.broadcasted_iota(jnp.int32, (BLOCK, BLOCK), 0) == lax.broadcasted_iota(
         jnp.int32, (BLOCK, BLOCK), 1
@@ -337,33 +374,42 @@
         x_copy(k, row).wait_send()
         c_copy(k, row).wait_send()
         r_copy(k, across).wait_send()
-        for copy in out_copies(k):
+        return carry
+
+    lax.fori_loop(0, chunks, last, 0)
+    for head in range(chunks // JOIN):
+        for copy in out_copies(head):
             copy.wait()
-        return carry
-
-    lax.fori_loop(0, chunks, last, 0)
     for slot, (e, d) in enumerate(same):
         peak_copy(slot, e, d).wait_send()
-    for d in range(n_ctx):
-        if d > 0:
-            rs_copy(d).wait_send()
-            ag_copy(d, ctx).wait_send()
-        gx_copy(d, row).wait_send()
-        gc_copy(d, row).wait_send()
-        gr_copy(d, across).wait_send()
+    for h in range(cuts):
+        for d in range(n_ctx):
+            if d > 0:
+                rs_copy(h, d).wait_send()
+                ag_copy(h, d, ctx).wait_send()
+            gx_copy(h, d, row).wait_send()
+            gc_copy(h, d, row).wait_send()
+            gr_copy(h, d, across).wait_send()
+
+
+def cuts_of(n_ctx):
+    piece = len(PAIRS) * BLOCK // (4 * n_ctx)
+    return CUTS if piece % (8 * CUTS) == 0 else 1
 
 
 def gather(grad, logit, n_ctx):
     _, rows, cols = grad.shape
-    chunks = cols // HEAD_COLS
+    chunks = cols // CHUNK
+    heads = cols // HEAD_COLS
+    cuts = cuts_of(n_ctx)
     f32, bf16 = jnp.float32, jnp.bfloat16
     sem = pltpu.SemaphoreType.DMA
     packed_rows = len(PAIRS) * BLOCK
     vmem = pl.BlockSpec(memory_space=pltpu.VMEM)
     anywhere = pl.BlockSpec(memory_space=pl.ANY)
-    wide = (chunks, KV_RANK, HEAD_COLS)
+    wide = (heads, KV_RANK, HEAD_COLS)
     return pl.pallas_call(
-        functools.partial(gather_kernel, n_ctx, chunks),
+        functools.partial(gather_kernel, n_ctx, chunks, cuts),
         out_shape=(
             jax.ShapeDtypeStruct(wide, bf16),
             jax.ShapeDtypeStruct(wide, bf16),
@@ -371,29 +417,31 @@
             jax.ShapeDtypeStruct((rows, KV_RANK), bf16),
             jax.ShapeDtypeStruct((8, 128), f32),
         ),
-        in_specs=[vmem, vmem],
+        in_specs=[anywhere, vmem],
         out_specs=(anywhere, anywhere, vmem, vmem, vmem),
         scratch_shapes=[
-            pltpu.VMEM((chunks, rows, HEAD_COLS), f32),
-            pltpu.VMEM((chunks, rows, HEAD_COLS), f32),
-            pltpu.VMEM(wide, f32),
+            pltpu.VMEM(grad.shape, bf16),
+            pltpu.VMEM((chunks, rows, CHUNK), f32),
+            pltpu.VMEM((chunks, rows, CHUNK), f32),
+            pltpu.VMEM((chunks, KV_RANK, CHUNK), f32),
             pltpu.VMEM(wide, bf16),
             pltpu.VMEM(wide, bf16),
             pltpu.VMEM((KV_RANK, KV_RANK), f32),
             pltpu.VMEM((KV_RANK, KV_RANK), f32),
             pltpu.VMEM((packed_rows, BLOCK), f32),
-            pltpu.VMEM((n_ctx, packed_rows // (4 * n_ctx), BLOCK), f32),
+            pltpu.VMEM((cuts * n_ctx, packed_rows // (4 * n_ctx * cuts), BLOCK), f32),
             pltpu.VMEM((packed_rows, BLOCK), f32),
             pltpu.VMEM((KV_RANK, KV_RANK), f32),
             pltpu.VMEM((8, 128), f32),
             pltpu.VMEM((2 * n_ctx - 1, 8, 128), f32),
         ]
         + [sem((chunks,))] * 8
-        + [sem((2, chunks))]
-        + [sem((n_ctx,))] * 10
-        + [sem((2 * n_ctx - 1,))] * 2,
+        + [sem((2, heads))]
+        + [sem((cuts * n_ctx,))] * 10
+        + [sem((2 * n_ctx - 1,))] * 2
+        + [sem((2,))],
         compiler_params=pltpu.CompilerParams(
-            collective_id=0, has_side_effects=True, vmem_limit_bytes=56 * 1024 * 1024
+            collective_id=0, has_side_effects=True, vmem_limit_bytes=36 * 1024 * 1024
         ),
     )(grad, logit)
 
@@ -425,12 +473,13 @@
         out_shape=(shape, shape),
         in_specs=[pl.BlockSpec(memory_space=pltpu.SMEM), whole, whole, stream, stream, flat],
         out_specs=(flat, flat),
+        compiler_params=pltpu.CompilerParams(vmem_limit_bytes=20 * 1024 * 1024),
     )(factor, t_high, t_low, x_high, x_low, weight)
 
 
 def kernel_shards(n_ctx, grad_parts, weight, logit_max):
     x_high, x_low, t_high, t_low, factor = gather(grad_parts[0], logit_max[0, 0], n_ctx)
-    return apply(factor, t_high, t_low, x_high, x_low, weight, 2)
+    return apply(factor, t_high, t_low, x_high, x_low, weight, 4)
 
 
 def solution(mesh):

time: 91.7 us -> 87.4 us (0.953)
  Pallas kernels: 90.7 us -> 84.3 us
  local copies, waits for them, and re-layouts: 0 us -> 2.27 us
    pallas_call x1, Pallas kernels: 9.17 us -> 4.44 us  [apply(): pl.pallas_call(functools.partial(apply_kernel, heads), grid=(chunks // he...]
    unnamed x0 -> x6, local copies, waits for them, and re-layouts: none -> 2.27 us
    pallas_call x1, Pallas kernels: 81.6 us -> 79.8 us  [gather(): pl.pallas_call(functools.partial(gather_kernel, n_ctx, chunks, cuts), out...]
where the time goes in v2:
time: 87.4 us; the launch traced here: 87.2 us
  Pallas kernels  84.3 us (96%)
  local copies, waits for them, and re-layouts  2.27 us (3%)
    pallas_call x1, Pallas kernels, gather(): pl.pallas_call(functools.partial(gather_kernel, n_ctx, chunks, cuts), out...  79.8 us
    pallas_call x1, Pallas kernels, apply(): pl.pallas_call(functools.partial(apply_kernel, heads), grid=(chunks // he...  4.44 us
    unnamed x6, local copies, waits for them, and re-layouts  2.27 us

profile of v2, /device:TPU:1, one launch (start us, length us, event | category | flops | bytes accessed | tf_op | source)
XLA Modules:
  0.0 87.2 jit_solution(14693348273932695571)
XLA Ops:
  0.6 0.0 copy-start
  0.6 1.6 %copy-done = bf16[1,2,128,4096]{3,2,1,0:T(8,128)(2,1)S(1)} copy-done((bf16[1,2,128,4096]{3,2,1,0:T(8,128)(2,1)S(1)}, bf16[1,2,128,4096]{3,2,1,0:T(8,128)(2,1)}, u32[]{:S(2)}) %copy-start) | copy-done | bytes 2097176
  2.2 0.0 copy-start.2
  2.2 0.7 copy-done.2
  2.9 0.0 copy-start.1
  2.9 79.8 %shard_map.50 = (bf16[16,512,256]{2,1,0:T(8,128)(2,1)S(1)}, bf16[16,512,256]{2,1,0:T(8,128)(2,1)S(1)}, bf16[128,512]{1,0:T(8,128)(2,1)S(1)}, bf16[128,512]{1,0:T(8,128)(2,1)S(1)}, f32[8,128]{1,0:T(8,128)S(1)}) custom-call(bf16[2,128,4096]{2,1,0:T(8,128)(2,1)S(1)} %bitcast.2, f32[2,64]{1,0:T(2,128)S(1)} %bitcast.3), custom_call_target="tpu_custom_call" | custom-call | tf_op jit(solution)/shard_map/pallas_call | solution.py:411
  82.7 0.0 copy-done.1
  82.7 4.4 %shard_map.51 = (f32[1,128,4096]{2,1,0:T(8,128)}, f32[1,128,4096]{2,1,0:T(8,128)}) custom-call(f32[8,128]{1,0:T(8,128)S(1)} %get-tuple-element.7.factor, bf16[128,512]{1,0:T(8,128)(2,1)S(1)} %get-tuple-element.8.t_high, bf16[128,512]{1,0:T(8,128)(2,1)S(1)} %get-tuple-element.9.t_low, bf16[16,512,256]{2,1,0:T(8,128)(2,1)S(1)} %get-tuple-element.10.x_high, ...), custom_call_target="tpu_custom_call" | custom-call | tf_op jit(solution)/shard_map/pallas_call | solution.py:470
Async XLA Ops:
  0.6 1.6 %copy-start = (bf16[1,2,128,4096]{3,2,1,0:T(8,128)(2,1)S(1)}, bf16[1,2,128,4096]{3,2,1,0:T(8,128)(2,1)}, u32[]{:S(2)}) copy-start(bf16[1,2,128,4096]{3,2,1,0:T(8,128)(2,1)} %param.3) | copy-start | bytes 6291460
  2.2 0.7 copy-start.2
  2.9 79.8 %copy-start.1 = (bf16[1,128,4096]{2,1,0:T(8,128)(2,1)S(1)}, bf16[1,128,4096]{2,1,0:T(8,128)(2,1)}, u32[]{:S(2)}) copy-start(bf16[1,128,4096]{2,1,0:T(8,128)(2,1)} %weight.1) | copy-start | bytes 3145732

commit v3 on v2

--- a/solution.py
+++ b/solution.py
@@ -105,7 +105,7 @@
 def gather_kernel(
     n_ctx, chunks, cuts,
     grad, logit, x_high, x_low, t_high, t_low, factor,
-    grads, outgoing, arriving, x_all, high_all, low_all, main, cross,
+    logits, grads, outgoing, arriving, x_all, high_all, low_all, main, cross,
     packed, partial, total, gram, own_peak, peaks,
     y_send, y_recv, x_send, x_recv, c_send, c_recv, r_send, r_recv, out_sem,
     rs_send, rs_recv, ag_send, ag_recv, gx_send, gx_recv, gc_send, gc_recv, gr_send, gr_recv,
@@ -123,6 +123,7 @@
         pltpu.make_async_copy(grad.at[layer], grads.at[layer], in_sem.at[i])
         for i, layer in enumerate((other_dp, dp))
     ]
+    loads.append(pltpu.make_async_copy(logit, logits, in_sem.at[2]))
     for load in loads:
         load.start()
 
@@ -148,8 +149,6 @@
     for f in (across, beside):
         pl.semaphore_signal(barrier, 1, device_id=device(dp, ctx, f), device_id_type=pl.DeviceIdType.MESH)
     own_peak[...] = jnp.full(own_peak.shape, 10.0, jnp.float32)
-    own_peak[0 : logit.shape[0], 0 : logit.shape[1]] = logit[...]
-    pl.semaphore_wait(barrier, len(same) + 2)
 
     def block_of(f):
         return pl.ds(pl.multiple_of(f * rows, rows), rows)
@@ -180,19 +179,20 @@
             pltpu.make_async_copy(low_all.at[k], x_low.at[k], out_sem.at[1, k]),
         )
 
-    def first(k, carry):
-        @pl.when(k < chunks)
-        def _():
-            outgoing[k] = grads[other_dp, :, columns(k)].astype(jnp.float32)
-
-        @pl.when(k >= 1)
-        def _():
-            y_copy(k - 1).start()
-
+    def fill(k, carry):
+        outgoing[k] = grads[other_dp, :, columns(k)].astype(jnp.float32)
         return carry
 
+    def push(k, carry):
+        y_copy(k).start()
+        return carry
+
     loads[0].wait()
-    lax.fori_loop(0, chunks + 1, first, 0)
+    lax.fori_loop(0, chunks, fill, 0)
+    loads[2].wait()
+    own_peak[0 : logit.shape[0], 0 : logit.shape[1]] = logits[...]
+    pl.semaphore_wait(barrier, len(same) + 2)
+    lax.fori_loop(0, chunks, push, 0)
 
     def peak_copy(slot, e, d):
         return send(own_peak, peaks.at[slot], pk_send.at[slot], pk_recv.at[slot], shifted(e, d))
@@ -407,6 +407,7 @@
     packed_rows = len(PAIRS) * BLOCK
     vmem = pl.BlockSpec(memory_space=pltpu.VMEM)
     anywhere = pl.BlockSpec(memory_space=pl.ANY)
+    hbm = pl.BlockSpec(memory_space=pltpu.HBM)
     wide = (heads, KV_RANK, HEAD_COLS)
     return pl.pallas_call(
         functools.partial(gather_kernel, n_ctx, chunks, cuts),
@@ -417,9 +418,10 @@
             jax.ShapeDtypeStruct((rows, KV_RANK), bf16),
             jax.ShapeDtypeStruct((8, 128), f32),
         ),
-        in_specs=[anywhere, vmem],
+        in_specs=[hbm, hbm],
         out_specs=(anywhere, anywhere, vmem, vmem, vmem),
         scratch_shapes=[
+            pltpu.VMEM(logit.shape, f32),
             pltpu.VMEM(grad.shape, bf16),
             pltpu.VMEM((chunks, rows, CHUNK), f32),
             pltpu.VMEM((chunks, rows, CHUNK), f32),
@@ -439,11 +441,11 @@
         + [sem((2, heads))]
         + [sem((cuts * n_ctx,))] * 10
         + [sem((2 * n_ctx - 1,))] * 2
-        + [sem((2,))],
+        + [sem((3,))],
         compiler_params=pltpu.CompilerParams(
             collective_id=0, has_side_effects=True, vmem_limit_bytes=36 * 1024 * 1024
         ),
-    )(grad, logit)
+    )(pltpu.with_memory_space_constraint(grad, pltpu.HBM), pltpu.with_memory_space_constraint(logit, pltpu.HBM))
 
 
 def apply_kernel(heads, factor, t_high, t_low, x_high, x_low, weight, update, fresh):

time: 87.4 us -> 84.9 us (0.971)
  local copies, waits for them, and re-layouts: 2.27 us -> 0.01 us
    unnamed x6 -> x2, local copies, waits for them, and re-layouts: 2.27 us -> 0.01 us
where the time goes in v3:
time: 84.9 us; the launch traced here: 84.8 us
  Pallas kernels  84.1 us (99%)
    pallas_call x1, Pallas kernels, gather(): pl.pallas_call(functools.partial(gather_kernel, n_ctx, chunks, cuts), out...  79.7 us
    pallas_call x1, Pallas kernels, apply(): pl.pallas_call(functools.partial(apply_kernel, heads), grid=(chunks // he...  4.44 us

profile of v3, /device:TPU:1, one launch (start us, length us, event | category | flops | bytes accessed | tf_op | source)
XLA Modules:
  0.0 84.8 jit_solution(4980612381352420513)
XLA Ops:
  0.6 0.0 copy-start
  0.6 79.7 %shard_map.50 = (bf16[16,512,256]{2,1,0:T(8,128)(2,1)S(1)}, bf16[16,512,256]{2,1,0:T(8,128)(2,1)S(1)}, bf16[128,512]{1,0:T(8,128)(2,1)S(1)}, bf16[128,512]{1,0:T(8,128)(2,1)S(1)}, f32[8,128]{1,0:T(8,128)S(1)}) custom-call(bf16[2,128,4096]{2,1,0:T(8,128)(2,1)} %bitcast.2, f32[2,64]{1,0:T(2,128)} %bitcast.3), custom_call_target="tpu_custom_call" | custom-call | tf_op jit(solution)/shard_map/pallas_call | solution.py:412
  80.3 0.0 copy-done
  80.3 4.4 %shard_map.51 = (f32[1,128,4096]{2,1,0:T(8,128)}, f32[1,128,4096]{2,1,0:T(8,128)}) custom-call(f32[8,128]{1,0:T(8,128)S(1)} %get-tuple-element.7.factor, bf16[128,512]{1,0:T(8,128)(2,1)S(1)} %get-tuple-element.8.t_high, bf16[128,512]{1,0:T(8,128)(2,1)S(1)} %get-tuple-element.9.t_low, bf16[16,512,256]{2,1,0:T(8,128)(2,1)S(1)} %get-tuple-element.10.x_high, ...), custom_call_target="tpu_custom_call" | custom-call | tf_op jit(solution)/shard_map/pallas_call | solution.py:472
Async XLA Ops:
  0.6 79.7 %copy-start = (bf16[1,128,4096]{2,1,0:T(8,128)(2,1)S(1)}, bf16[1,128,4096]{2,1,0:T(8,128)(2,1)}, u32[]{:S(2)}) copy-start(bf16[1,128,4096]{2,1,0:T(8,128)(2,1)} %weight.1) | copy-start | bytes 3145732

commit v4 on v3

--- a/solution.py
+++ b/solution.py
@@ -25,7 +25,7 @@
 
 HEAD_COLS = NOPE + V_DIM
 BLOCK = 128
-CHUNK = 128
+CHUNK = 256
 CUTS = 2
 JOIN = HEAD_COLS // CHUNK
 SIDE = KV_RANK // BLOCK

time: 84.9 us -> 83.7 us (0.986)
  Pallas kernels: 84.1 us -> 82.9 us
    pallas_call x1, Pallas kernels: 79.7 us -> 78.4 us  [gather(): pl.pallas_call(functools.partial(gather_kernel, n_ctx, chunks, cuts), out...]
where the time goes in v4:
time: 83.7 us; the launch traced here: 83.5 us
  Pallas kernels  82.9 us (99%)
    pallas_call x1, Pallas kernels, gather(): pl.pallas_call(functools.partial(gather_kernel, n_ctx, chunks, cuts), out...  78.4 us
    pallas_call x1, Pallas kernels, apply(): pl.pallas_call(functools.partial(apply_kernel, heads), grid=(chunks // he...  4.44 us

profile of v4, /device:TPU:1, one launch (start us, length us, event | category | flops | bytes accessed | tf_op | source)
XLA Modules:
  0.0 83.5 jit_solution(9046658278983334135)
XLA Ops:
  0.6 0.0 copy-start
  0.6 78.4 %shard_map.50 = (bf16[16,512,256]{2,1,0:T(8,128)(2,1)S(1)}, bf16[16,512,256]{2,1,0:T(8,128)(2,1)S(1)}, bf16[128,512]{1,0:T(8,128)(2,1)S(1)}, bf16[128,512]{1,0:T(8,128)(2,1)S(1)}, f32[8,128]{1,0:T(8,128)S(1)}) custom-call(bf16[2,128,4096]{2,1,0:T(8,128)(2,1)} %bitcast.2, f32[2,64]{1,0:T(2,128)} %bitcast.3), custom_call_target="tpu_custom_call" | custom-call | tf_op jit(solution)/shard_map/pallas_call | solution.py:412
  79.1 0.0 copy-done
  79.1 4.4 %shard_map.51 = (f32[1,128,4096]{2,1,0:T(8,128)}, f32[1,128,4096]{2,1,0:T(8,128)}) custom-call(f32[8,128]{1,0:T(8,128)S(1)} %get-tuple-element.7.factor, bf16[128,512]{1,0:T(8,128)(2,1)S(1)} %get-tuple-element.8.t_high, bf16[128,512]{1,0:T(8,128)(2,1)S(1)} %get-tuple-element.9.t_low, bf16[16,512,256]{2,1,0:T(8,128)(2,1)S(1)} %get-tuple-element.10.x_high, ...), custom_call_target="tpu_custom_call" | custom-call | tf_op jit(solution)/shard_map/pallas_call | solution.py:472
Async XLA Ops:
  0.6 78.5 %copy-start = (bf16[1,128,4096]{2,1,0:T(8,128)(2,1)S(1)}, bf16[1,128,4096]{2,1,0:T(8,128)(2,1)}, u32[]{:S(2)}) copy-start(bf16[1,128,4096]{2,1,0:T(8,128)(2,1)} %weight.1) | copy-start | bytes 3145732
